TPU v7x, 32 devices: a whole 2x2x4 slice. The times are simulated.
32 devices in a mesh: mem: 8 (over z, y), band: 4 (over x, core).
Axes of the slice: x: 2, y: 2, z: 4, core: 2. Of those that a mesh axis runs over, the one named last changes fastest.
Arguments:
- alpha: bfloat16 [16, 4, 320, 720], P('mem', None, 'band'), may hold values from -6 to 6
- static_ctl: bfloat16 [4, 320, 720], P(None, 'band'), may hold values from -6 to 6
- perturbations: bfloat16 [16, 4, 320, 720], P('mem', None, None, 'band'), may hold values from -6 to 6
- static_std: float32 [4, 320, 720], P(None, None, 'band'), may hold values from 0.5 to 2
- lon_root: bfloat16 [720, 720], replicated, may hold values from -0.11 to 1.11
- lat_root: bfloat16 [320, 320], replicated, may hold values from -0.11 to 1.11
- jacobian: bfloat16 [32, 4, 320, 720], P(None, None, 'mem', 'band'), may hold values from -3 to 3
- obs_count: int32 [320, 720], P('mem', 'band'), may hold values from 1 to 6
- channel_mask: int32 [32, 320, 720], P(None, 'mem', 'band'), may hold values 0 or 1
- channel_error: float32 [32], replicated, may hold values from 1 to 2
- member_weight: int32 [16], replicated, may hold values from 1 to 4
Outputs:
- grad_alpha: float32 [16, 4, 320, 720], P('mem', None, 'band')
- grad_static: float32 [4, 320, 720], P(None, 'band')
All inputs are finite; a program needn't handle non-finite values. No bound on the sum of `channel_mask` on one device may be relied on, other than what follows from the above.
Results may differ from a plain program's by a relative error of at most 0.0055.
Values may be sent and summed in bfloat16 or wider, within the bound.
No kernel may reach another device: no remote copies, remote signals or barrier semaphores. Data moves between devices by JAX's collectives and lax.ppermute only.
A program may use at most 64 MiB of HBM per device.

v0:
```python
import jax
import jax.numpy as jnp
from jax import lax
from jax.sharding import PartitionSpec as P


def shards(
    alpha,
    static_ctl,
    perturbations,
    static_std,
    lon_root,
    lat_root,
    jacobian,
    obs_count,
    channel_mask,
    channel_error,
    member_weight,
):
    members = alpha.shape[0]
    rows = jacobian.shape[2]
    rank = lax.axis_index("mem")
    weights = member_weight.astype(jnp.float32)
    coef = weights / jnp.sqrt(jnp.sum(weights * weights))
    own_coef = lax.dynamic_slice_in_dim(coef, rank * members, members, 0)
    fields = jnp.concatenate([alpha, static_ctl[None]], axis=0)
    along_lon = jnp.dot(fields, lon_root, preferred_element_type=jnp.float32).astype(jnp.bfloat16)
    regrouped = lax.all_to_all(along_lon, "band", split_axis=3, concat_axis=2, tiled=True)
    member_lat = jnp.einsum(
        "ij,msjk->msik", lat_root, regrouped[:members], preferred_element_type=jnp.float32
    )
    own_root = lax.dynamic_slice_in_dim(lat_root, rank * rows, rows, 0)
    own_static = jnp.einsum(
        "ij,sjk->sik", own_root, regrouped[members], preferred_element_type=jnp.float32
    )
    scaled = 0.8 * own_coef
    ensemble_term = jnp.sum(
        scaled[:, None, None, None] * perturbations.astype(jnp.float32) * member_lat, axis=0
    )
    summed = lax.psum(ensemble_term, "mem")
    own_sum = lax.dynamic_slice_in_dim(summed, rank * rows, rows, 1)
    own_std = lax.dynamic_slice_in_dim(static_std, rank * rows, rows, 1)
    increment = own_sum + 0.6 * own_std * own_static
    obs_weight = (
        channel_mask.astype(jnp.float32)
        * obs_count.astype(jnp.float32)[None]
        / (channel_error * channel_error)[:, None, None]
    )
    jac_full = jacobian.astype(jnp.float32)
    radiance = jnp.sum(jac_full * increment[None], axis=1)
    obs_gradient = jnp.sum(jac_full * (obs_weight * radiance)[:, None], axis=0).astype(jnp.bfloat16)
    band_gradient = lax.all_gather(obs_gradient, "mem", axis=1, tiled=True).astype(jnp.float32)
    member_adjoint = (
        scaled[:, None, None, None] * perturbations.astype(jnp.float32) * band_gradient[None]
    ).astype(jnp.bfloat16)
    static_adjoint = (0.6 * static_std * band_gradient).astype(jnp.bfloat16)
    adjoints = jnp.concatenate([member_adjoint, static_adjoint[None]], axis=0)
    back_lat = jnp.einsum(
        "ji,msjk->msik", lat_root, adjoints, preferred_element_type=jnp.float32
    ).astype(jnp.bfloat16)
    returned = lax.all_to_all(back_lat, "band", split_axis=2, concat_axis=3, tiled=True)
    back_lon = jnp.einsum("msil,jl->msij", returned, lon_root, preferred_element_type=jnp.float32)
    grad_alpha = alpha.astype(jnp.float32) + back_lon[:members]
    grad_static = static_ctl.astype(jnp.float32) + back_lon[members]
    return (grad_alpha, grad_static)


def solution(mesh):
    in_specs = (
        P("mem", None, "band", None),
        P(None, "band", None),
        P("mem", None, None, "band"),
        P(None, None, "band"),
        P(),
        P(),
        P(None, None, "mem", "band"),
        P("mem", "band"),
        P(None, "mem", "band"),
        P(),
        P(),
    )
    out_specs = (P("mem", None, "band", None), P(None, "band", None))
    return jax.shard_map(shards, mesh=mesh, in_specs=in_specs, out_specs=out_specs, check_vma=False)
```

profile of v0, /device:TPU:0, one launch (start us, length us, event | category | flops | bytes accessed | tf_op | source)
XLA Modules:
  0.0 232.6 jit_solution(4130602733582369304)
XLA Ops:
  7.2 0.0 copy-start
  7.2 1.2 copy-done
  8.4 2.7 %convolution_convert_fusion.1 = bf16[3,4,80,720]{3,2,1,0:T(8,128)(2,1)S(1)} fusion(bf16[1,4,80,720]{3,2,1,0:T(8,128)(2,1)} %bitcast.52, bf16[2,4,80,720]{3,2,1,0:T(8,128)(2,1)} %param.11, bf16[720,720]{1,0:T(8,128)(2,1)S(1)} %copy-done), kind=kOutput, calls=%fused_computation.13 | convolution fusion | flops 996710400 | bytes 3801600 | tf_op jit(solution)/shard_map/dot_general | solution.py:27
  11.1 3.3 %copy.28 = bf16[3,4,80,720]{2,1,0,3:T(4,128)(2,1)} copy(bf16[3,4,80,720]{3,2,1,0:T(8,128)(2,1)S(1)} %convolution_convert_fusion.1) | data formatting | bytes 2764800 | tf_op jit(solution)/shard_map/convert_element_type | solution.py:27
  14.4 0.0 copy-start.11
  14.4 4.4 %all-to-all-start = ((bf16[3,4,80,720]{2,1,0,3:T(4,128)(2,1)}), bf16[3,4,80,720]{2,1,0,3:T(4,128)(2,1)S(1)}, u32[]{:S(2)}, u32[]{:S(2)}) async-start(bf16[3,4,80,720]{2,1,0,3:T(4,128)(2,1)} %copy.28), calls=%async_computation | async-start | bytes 4423680 | tf_op jit(solution)/shard_map/all_to_all | solution.py:28
  18.7 0.0 all-reduce.2.cloned.1.call-start
  18.7 0.0 copy-done.11
  18.7 0.6 multiply_reduce_fusion
  20.0 0.1 dynamic-slice_multiply_fusion
  20.1 25.5 %all-to-all-done = bf16[3,4,80,720]{2,1,0,3:T(4,128)(2,1)S(1)} async-done(((bf16[3,4,80,720]{2,1,0,3:T(4,128)(2,1)}), bf16[3,4,80,720]{2,1,0,3:T(4,128)(2,1)S(1)}, u32[]{:S(2)}, u32[]{:S(2)}) %all-to-all-start) | async-done | bytes 1382432 | tf_op jit(solution)/shard_map/all_to_all | solution.py:28
  45.6 3.8 %copy.29 = bf16[3,4,80,4,180]{4,2,3,1,0:T(8,128)(2,1)} copy(bf16[3,4,80,4,180]{2,1,0,4,3:T(4,128)(2,1)S(1)} %bitcast.46) | data formatting | bytes 2764800 | tf_op jit(solution)/shard_map/all_to_all | solution.py:28
  49.4 0.0 copy-start.4
  49.4 0.0 copy-start.9
  49.4 1.5 slice.21
  50.9 0.1 copy-done.4
  51.0 0.0 copy-done.9
  51.1 1.4 fusion.2
  52.4 0.0 copy-start.12
  52.4 0.0 copy-start.8
  52.5 0.0 copy-start.2
  52.5 1.5 copy.31
  54.0 0.0 all-reduce.2.cloned.1.call-update
  54.0 0.0 copy-done.12
  54.1 0.0 copy-done.8
  54.1 0.0 copy-done.2
  54.1 0.3 constant_dynamic-slice_fusion
  54.3 0.2 copy.44
  54.6 1.1 slice.22
  55.7 83.2 %all-reduce.2.cloned.1.call-done = f32[4,320,180]{2,1,0:T(8,128)} async-done(((f32[4,320,180]{2,1,0:T(8,128)}), f32[4,320,180]{2,1,0:T(8,128)}) %all-reduce.2.cloned.1.call-update) | async-done | bytes 921616 | tf_op jit(solution)/shard_map/psum | solution.py:40
  138.9 1.2 fusion.13
  140.1 0.0 copy-start.3
  140.1 2.6 %fusion = f32[32,40,180]{2,1,0:T(8,128)S(1)} fusion(bf16[32,4,40,180]{3,2,1,0:T(8,128)(2,1)} %param.17, f32[4,40,180]{2,1,0:T(8,128)S(1)} %fusion.13), kind=kLoop, calls=%fused_computation.2 | loop fusion | flops 2534400 | bytes 2880000 | tf_op jit(solution)/shard_map/reduce_sum | solution.py:50
  142.7 0.0 copy-done.3
  142.8 0.0 copy-start.1
  142.8 0.2 divide_multiply_fusion
  143.0 1.5 copy-done.1
  144.5 0.7 fusion.1
  145.2 31.8 %all_gather.3 = bf16[4,320,180]{2,0,1:T(4,128)(2,1)S(1)} all-gather(bf16[4,40,180]{2,0,1:T(4,128)(2,1)S(1)} %copy.34), channel_id=1, replica_groups=mesh['mem'=8,'band'=4] {'mem'}, dimensions={1}, use_global_device_ids=true | all-gather | bytes 518400 | tf_op jit(solution)/shard_map/all_gather | solution.py:52
  177.0 0.9 copy.35
  177.8 0.0 copy-start.5
  177.9 0.2 fusion.20
  178.0 0.1 convert_element_type.51
  178.1 1.0 copy-done.5
  179.1 0.0 copy-start.10
  179.1 0.4 multiply_convert_fusion
  179.5 0.6 copy-done.10
  180.0 2.5 %fusion.6 = bf16[3,4,320,180]{2,3,1,0:T(8,128)(2,1)} fusion(bf16[1,4,320,180]{2,3,1,0:T(8,128)(2,1)S(1)} %fusion.20, bf16[2,4,320,180]{2,3,1,0:T(8,128)(2,1)S(1)} %multiply_convert_fusion, bf16[320,320]{1,0:T(8,128)(2,1)S(1)} %copy-done.10), kind=kOutput, calls=%fused_computation.14 | convolution fusion | flops 443750400 | bytes 2969600 | tf_op jit(solution)/shard_map/ji,msjk->msik/dot_general | solution.py:58
  182.6 6.7 %copy.37 = bf16[3,4,320,180]{3,1,0,2:T(4,128)(2,1)S(1)} copy(bf16[3,4,320,180]{2,3,1,0:T(8,128)(2,1)} %fusion.6) | data formatting | bytes 2764800 | tf_op jit(solution)/shard_map/convert_element_type | solution.py:60
  189.2 26.8 %all_to_all.33 = bf16[3,4,320,180]{3,1,0,2:T(4,128)(2,1)S(1)} all-to-all(bf16[3,4,320,180]{3,1,0,2:T(4,128)(2,1)S(1)} %copy.37), channel_id=1, replica_groups=mesh['mem'=8,'band'=4] {'band'}, dimensions={2} | all-to-all | bytes 2764800 | tf_op jit(solution)/shard_map/all_to_all | solution.py:61
  216.0 0.3 copy.38
  216.3 1.0 copy.39
  217.4 2.5 %all_to_all.30 = bf16[3,4,80,720]{3,2,1,0:T(8,128)(2,1)} reshape(bf16[3,4,80,4,180]{4,3,2,1,0:T(4,128)(2,1)S(1)} %copy.39) | data formatting | bytes 2764800 | tf_op jit(solution)/shard_map/all_to_all | solution.py:61
  219.9 0.0 copy-start.7
  219.9 2.8 %fusion.16 = f32[3,4,80,720]{3,2,1,0:T(8,128)S(1)} fusion(bf16[3,4,80,720]{3,2,1,0:T(8,128)(2,1)} %all_to_all.30, bf16[720,720]{1,0:T(8,128)(2,1)S(1)} %copy-done), kind=kOutput, calls=%fused_computation.25 | convolution fusion | flops 995328000 | bytes 5184000 | tf_op jit(solution)/shard_map/msil,jl->msij/dot_general | solution.py:62
  222.7 0.0 copy-done.7
  222.7 0.0 copy-start.6
  222.7 1.0 fusion.19
  223.7 0.5 copy-done.6
  224.2 1.5 slice_add_fusion
  (4 shorter events, 0.0 us)
Async XLA Ops:
  7.2 1.3 copy-start
  14.4 4.4 %copy-start.11 = (s32[16]{0:T(128)S(1)}, s32[16]{0:T(128)}, u32[]{:S(2)}) copy-start(s32[16]{0:T(128)} %param.21) | copy-start | bytes 196
  14.4 31.3 %all-to-all-start = ((bf16[3,4,80,720]{2,1,0,3:T(4,128)(2,1)}), bf16[3,4,80,720]{2,1,0,3:T(4,128)(2,1)S(1)}, u32[]{:S(2)}, u32[]{:S(2)}) async-start(bf16[3,4,80,720]{2,1,0,3:T(4,128)(2,1)} %copy.28), calls=%async_computation | async-start | bytes 4423680 | tf_op jit(solution)/shard_map/all_to_all | solution.py:28
  18.7 120.2 %all-reduce.2.cloned.1.call-start = ((), (), s32[]{:S(2)}) async-start(), calls=%async_computation.2 | async-start | bytes 2621440 | tf_op jit(solution)/shard_map/psum | solution.py:40
  49.4 1.6 copy-start.4
  49.4 1.7 copy-start.9
  52.4 1.6 copy-start.12
  52.4 1.6 copy-start.8
  52.5 1.6 copy-start.2
  140.1 2.7 %copy-start.3 = (s32[32,40,180]{2,1,0:T(8,128)S(1)}, s32[32,40,180]{2,1,0:T(8,128)}, u32[]{:S(2)}) copy-start(s32[32,40,180]{2,1,0:T(8,128)} %param.19) | copy-start | bytes 2764804
  142.8 1.7 copy-start.1
  177.8 1.2 copy-start.5
  179.1 0.9 copy-start.10
  219.9 2.8 %copy-start.7 = (bf16[4,80,720]{2,1,0:T(8,128)(2,1)S(1)}, bf16[4,80,720]{2,1,0:T(8,128)(2,1)}, u32[]{:S(2)}) copy-start(bf16[4,80,720]{2,1,0:T(8,128)(2,1)} %param.12) | copy-start | bytes 1382404
  222.7 1.6 copy-start.6
Sparse Core Ops, SparseCore 0:
  54.1 84.7 all-reduce.1
where the time goes:
time: 233 us
  waiting for transfers between devices  109 us (47%)
  blocking collectives  58.6 us (25%)
  local copies, waits for them, and re-layouts  28 us (12%)
  between operations  15 us (6%)
  matrix products  10.5 us (5%)
  other arithmetic  7.4 us (3%)
  starting transfers between devices  4.37 us (2%)
    psum x1, waiting for transfers between devices, shards(): summed = lax.psum(ensemble_term, 'mem')  83.2 us
    all_gather x1, blocking collectives, shards(): lax.all_gather(obs_gradient, 'mem', axis=1, tiled=True).astype(jnp.float32)  31.8 us
    all_to_all x1, blocking collectives, shards(): lax.all_to_all(back_lat, 'band', split_axis=2, concat_axis=3, tiled=True)  26.8 us
    all_to_all x1, waiting for transfers between devices, shards(): lax.all_to_all(along_lon, 'band', split_axis=3, concat_axis=2, tiled=True)  25.5 us
    convert_element_type x1, local copies, waits for them, and re-layouts, shards(): back_lat = jnp.einsum('ji,msjk->msik', lat_root, adjoints, preferred_elem...  6.66 us
    unnamed x27, local copies, waits for them, and re-layouts  5.19 us
  transfers between devices with their start and end apart: 2, of which 2 were waited for; matrix products, arithmetic and copies ran while one was open for 1% of the time, Pallas kernels for 0%

commit v1 on v0

--- a/solution.py
+++ b/solution.py
@@ -37,7 +37,8 @@
     ensemble_term = jnp.sum(
         scaled[:, None, None, None] * perturbations.astype(jnp.float32) * member_lat, axis=0
     )
-    summed = lax.psum(ensemble_term, "mem")
+    parts = lax.all_gather(ensemble_term, "mem", axis=0, tiled=False)
+    summed = parts.sum(axis=0)
     own_sum = lax.dynamic_slice_in_dim(summed, rank * rows, rows, 1)
     own_std = lax.dynamic_slice_in_dim(static_std, rank * rows, rows, 1)
     increment = own_sum + 0.6 * own_std * own_static

time: 233 us -> 286 us (1.23)
  waiting for transfers between devices: 109 us -> 156 us
  other arithmetic: 7.4 us -> 11.6 us
    all_gather x0 -> x1, waiting for transfers between devices: none -> 131 us  [shards(): parts = lax.all_gather(ensemble_term, 'mem', axis=0, tiled=False)]
    psum x1 -> x0, waiting for transfers between devices: 83.2 us -> none  [shards(): summed = lax.psum(ensemble_term, 'mem')]
    reduce_sum x0 -> x1, other arithmetic: none -> 4.24 us  [shards(): summed = parts.sum(axis=0)]
where the time goes in v1:
time: 286 us
  waiting for transfers between devices  156 us (55%)
  blocking collectives  58.8 us (21%)
  local copies, waits for them, and re-layouts  27.9 us (10%)
  between operations  14.9 us (5%)
  other arithmetic  11.6 us (4%)
  matrix products  11.3 us (4%)
  starting transfers between devices  4.37 us (2%)
    all_gather x1, waiting for transfers between devices, shards(): parts = lax.all_gather(ensemble_term, 'mem', axis=0, tiled=False)  131 us
    all_gather x1, blocking collectives, shards(): lax.all_gather(obs_gradient, 'mem', axis=1, tiled=True).astype(jnp.float32)  32 us
    all_to_all x1, blocking collectives, shards(): lax.all_to_all(back_lat, 'band', split_axis=2, concat_axis=3, tiled=True)  26.8 us
    all_to_all x1, waiting for transfers between devices, shards(): lax.all_to_all(along_lon, 'band', split_axis=3, concat_axis=2, tiled=True)  25.5 us
    convert_element_type x1, local copies, waits for them, and re-layouts, shards(): back_lat = jnp.einsum('ji,msjk->msik', lat_root, adjoints, preferred_elem...  6.66 us
  transfers between devices with their start and end apart: 2, of which 2 were waited for; matrix products, arithmetic and copies ran while one was open for 1% of the time, Pallas kernels for 0%

profile of v1, /device:TPU:0, one launch (start us, length us, event | category | flops | bytes accessed | tf_op | source)
XLA Modules:
  0.0 285.5 jit_solution(7295096636082831438)
XLA Ops:
  7.2 0.0 copy-start
  7.2 1.2 copy-done
  8.4 2.7 convolution_convert_fusion.1
  11.1 3.3 %copy.40 = bf16[3,4,80,720]{2,1,0,3:T(4,128)(2,1)} copy(bf16[3,4,80,720]{3,2,1,0:T(8,128)(2,1)S(1)} %convolution_convert_fusion.1) | data formatting | bytes 2764800 | tf_op jit(solution)/shard_map/convert_element_type | solution.py:27
  14.4 0.0 copy-start.11
  14.4 4.4 %all-to-all-start = ((bf16[3,4,80,720]{2,1,0,3:T(4,128)(2,1)}), bf16[3,4,80,720]{2,1,0,3:T(4,128)(2,1)S(1)}, u32[]{:S(2)}, u32[]{:S(2)}) async-start(bf16[3,4,80,720]{2,1,0,3:T(4,128)(2,1)} %copy.40), calls=%async_computation | async-start | bytes 4423680 | tf_op jit(solution)/shard_map/all_to_all | solution.py:28
  18.7 0.0 all-gather.3.cloned.1.call-start
  18.7 0.0 copy-done.11
  18.7 0.6 multiply_reduce_fusion
  20.0 0.1 dynamic-slice_multiply_fusion
  20.1 25.5 %all-to-all-done = bf16[3,4,80,720]{2,1,0,3:T(4,128)(2,1)S(1)} async-done(((bf16[3,4,80,720]{2,1,0,3:T(4,128)(2,1)}), bf16[3,4,80,720]{2,1,0,3:T(4,128)(2,1)S(1)}, u32[]{:S(2)}, u32[]{:S(2)}) %all-to-all-start) | async-done | bytes 1382432 | tf_op jit(solution)/shard_map/all_to_all | solution.py:28
  45.6 3.8 %copy.41 = bf16[3,4,80,4,180]{4,2,3,1,0:T(8,128)(2,1)} copy(bf16[3,4,80,4,180]{2,1,0,4,3:T(4,128)(2,1)S(1)} %bitcast.48) | data formatting | bytes 2764800 | tf_op jit(solution)/shard_map/all_to_all | solution.py:28
  49.4 0.0 copy-start.4
  49.4 0.0 copy-start.9
  49.4 1.5 slice.21
  50.9 0.1 copy-done.4
  51.0 0.0 copy-done.9
  51.1 0.0 copy-start.12
  51.1 0.0 copy-start.8
  51.1 2.4 fusion.2
  53.4 0.0 all-gather.3.cloned.1.call-update
  53.5 0.0 copy-done.12
  53.5 0.0 copy-done.8
  53.5 1.4 constant_dynamic-slice_fusion
  54.9 0.2 copy.57
  55.1 1.1 slice.22
  56.2 131.0 %all-gather.3.cloned.1.call-done = f32[32,320,180]{1,2,0:T(8,128)} async-done(((f32[4,320,180]{1,2,0:T(8,128)}), f32[32,320,180]{1,2,0:T(8,128)}) %all-gather.3.cloned.1.call-update) | async-done | bytes 7372816 | tf_op jit(solution)/shard_map/all_gather | solution.py:40
  187.2 4.2 %reduce_sum.47 = f32[4,320,180]{1,2,0:T(8,128)S(1)} reduce(f32[8,4,320,180]{2,3,1,0:T(8,128)} %bitcast.47, f32[]{:T(128)} %constant.10.clone.1), dimensions={0}, to_apply=%region_2.0 | reduce | flops 1612800 | bytes 8294404 | tf_op jit(solution)/shard_map/reduce_sum | solution.py:41
  191.4 0.2 constant_dynamic-slice_fusion.1
  191.6 0.2 copy.56
  191.8 1.0 fusion.13
  192.8 0.0 copy-start.3
  192.8 2.6 fusion
  195.4 0.0 copy-done.3
  195.5 0.0 copy-start.1
  195.5 0.2 divide_multiply_fusion
  195.7 1.5 copy-done.1
  197.2 0.7 fusion.1
  197.9 0.0 copy-start.2
  197.9 32.0 %all_gather.11 = bf16[4,320,180]{2,0,1:T(4,128)(2,1)S(1)} all-gather(bf16[4,40,180]{2,0,1:T(4,128)(2,1)S(1)} %copy.46), channel_id=1, replica_groups=mesh['mem'=8,'band'=4] {'mem'}, dimensions={1}, use_global_device_ids=true | all-gather | bytes 518400 | tf_op jit(solution)/shard_map/all_gather | solution.py:53
  229.9 0.9 copy.47
  230.8 0.0 copy-done.2
  230.8 0.0 copy-start.5
  230.8 0.2 fusion.20
  231.0 0.1 convert_element_type.51
  231.1 1.0 copy-done.5
  232.0 0.0 copy-start.10
  232.0 0.4 multiply_convert_fusion
  232.4 0.6 copy-done.10
  233.0 2.5 fusion.6
  235.5 6.7 %copy.49 = bf16[3,4,320,180]{3,1,0,2:T(4,128)(2,1)S(1)} copy(bf16[3,4,320,180]{2,3,1,0:T(8,128)(2,1)} %fusion.6) | data formatting | bytes 2764800 | tf_op jit(solution)/shard_map/convert_element_type | solution.py:61
  242.2 26.8 %all_to_all.33 = bf16[3,4,320,180]{3,1,0,2:T(4,128)(2,1)S(1)} all-to-all(bf16[3,4,320,180]{3,1,0,2:T(4,128)(2,1)S(1)} %copy.49), channel_id=1, replica_groups=mesh['mem'=8,'band'=4] {'band'}, dimensions={2} | all-to-all | bytes 2764800 | tf_op jit(solution)/shard_map/all_to_all | solution.py:62
  269.0 0.3 copy.50
  269.3 1.0 copy.51
  270.3 2.5 all_to_all.30
  272.8 0.0 copy-start.7
  272.8 2.8 fusion.16
  275.6 0.0 copy-done.7
  275.6 0.0 copy-start.6
  275.6 1.0 fusion.19
  276.7 0.5 copy-done.6
  277.2 1.5 slice_add_fusion
  (4 shorter events, 0.0 us)
Async XLA Ops:
  7.2 1.3 copy-start
  14.4 4.4 %copy-start.11 = (s32[16]{0:T(128)S(1)}, s32[16]{0:T(128)}, u32[]{:S(2)}) copy-start(s32[16]{0:T(128)} %param.21) | copy-start | bytes 196
  14.4 31.3 %all-to-all-start = ((bf16[3,4,80,720]{2,1,0,3:T(4,128)(2,1)}), bf16[3,4,80,720]{2,1,0,3:T(4,128)(2,1)S(1)}, u32[]{:S(2)}, u32[]{:S(2)}) async-start(bf16[3,4,80,720]{2,1,0,3:T(4,128)(2,1)} %copy.40), calls=%async_computation | async-start | bytes 4423680 | tf_op jit(solution)/shard_map/all_to_all | solution.py:28
  18.7 168.5 %all-gather.3.cloned.1.call-start = ((), (), s32[]{:S(2)}) async-start(), calls=%async_computation.2 | async-start | bytes 10174464 | tf_op jit(solution)/shard_map/all_gather | solution.py:40
  49.4 1.6 copy-start.4
  49.4 1.7 copy-start.9
  51.1 2.4 copy-start.12
  51.1 2.4 copy-start.8
  192.8 2.7 copy-start.3
  195.5 1.7 copy-start.1
  197.9 32.9 %copy-start.2 = (f32[4,320,180]{1,0,2:T(4,128)S(1)}, f32[4,320,180]{1,0,2:T(4,128)}, u32[]{:S(2)}) copy-start(f32[4,320,180]{1,0,2:T(4,128)} %param.14) | copy-start | bytes 2764804
  230.8 1.2 copy-start.5
  232.0 0.9 copy-start.10
  272.8 2.8 copy-start.7
  275.6 1.6 copy-start.6
Sparse Core Ops, SparseCore 0:
  53.6 133.5 all-gather.2
